TPU v7x, 32 devices: a whole 2x2x4 slice. The times are simulated.
32 devices in a mesh: dp: 4 (over y, x), context: 8 (over z, core).
Axes of the slice: x: 2, y: 2, z: 4, core: 2. Of those that a mesh axis runs over, the one named last changes fastest.
Arguments:
- projected: bfloat16 [4096, 6144], P(('dp', 'context')), may hold values from -6 to 6
- short_taps: float32 [3, 6144], replicated, may hold values from -4 to 4
- long_filter: float32 [2048, 1024], P('context'), may hold values from -1.5 to 1.5
- skip_gain: float32 [2048], P('context'), may hold values from -4 to 4
- out_proj: bfloat16 [2048, 2048], P('dp'), may hold values from -0.125 to 0.125
- cotangent: bfloat16 [4096, 2048], P(('dp', 'context')), may hold values from -25 to 25
Outputs:
- grad_inputs: bfloat16 [4096, 6144], P(('dp', 'context'))
- grad_taps: float32 [3, 6144], replicated
- grad_filter: float32 [2048, 1024], P('context', 'dp')
- grad_skip: float32 [2048], P('context')
- grad_proj: float32 [2048, 2048], P(('dp', 'context'))
All inputs are finite; a program needn't handle non-finite values.
Results may differ from a plain program's by a relative error of at most 0.012.
Values may be sent and summed in bfloat16 or wider, within the bound.
No kernel may reach another device: no remote copies, remote signals or barrier semaphores. Data moves between devices by JAX's collectives and lax.ppermute only.
A program may use at most 128 MiB of HBM per device.

v0:
```python
import math
import jax
import jax.numpy as jnp
from jax import lax
from jax.sharding import PartitionSpec as P

PRECISE = lax.Precision.HIGH


def passed_along(value, axis, steps):
    count = lax.axis_size(axis)
    initial, last = (max(0, -steps), min(count, count - steps))
    return lax.ppermute(value, axis, [(source, source + steps) for source in range(initial, last)])


def angle_table(first_count, second_count, period):
    first_idx = lax.broadcasted_iota(jnp.int32, (first_count, second_count), 0)
    second_idx = lax.broadcasted_iota(jnp.int32, (first_count, second_count), 1)
    phases = first_idx * second_idx % period
    angles = phases.astype(jnp.float32) * (-2.0 * math.pi / period)
    return (jnp.cos(angles), jnp.sin(angles))


def make_tables(seq_len):
    radix_size = min(128, seq_len)
    blocks = 2 * seq_len // radix_size
    half_blocks = blocks // 2
    outer_re, outer_im = angle_table(blocks, blocks, blocks)
    twist = angle_table(blocks, radix_size, blocks * radix_size)
    inner_re, inner_im = angle_table(radix_size, radix_size, radix_size)
    first_table = jnp.concatenate([outer_re[:, :half_blocks], outer_im[:, :half_blocks]], 0)
    inner_fwd = jnp.concatenate(
        [jnp.concatenate([inner_re, inner_im], 1), jnp.concatenate([-inner_im, inner_re], 1)], 0
    )
    inner_back = jnp.concatenate(
        [jnp.concatenate([inner_re, -inner_im], 1), jnp.concatenate([inner_im, inner_re], 1)], 0
    )
    last_table = jnp.concatenate([outer_re[:half_blocks, :], outer_im[:half_blocks, :]], 1)
    return (first_table, twist, inner_fwd, inner_back, last_table)


def forward_spectrum(signal, tables):
    first_table, (twist_re, twist_im), inner_fwd, inner_back, last_table = tables
    blocks = twist_re.shape[0]
    radix_size = twist_re.shape[1]
    shaped = signal.reshape(signal.shape[0], blocks // 2, radix_size)
    first = jnp.einsum("kn,cnm->ckm", first_table, shaped, precision=PRECISE)
    first_re = first[:, :blocks]
    first_im = first[:, blocks:]
    turned = jnp.concatenate(
        [first_re * twist_re - first_im * twist_im, first_re * twist_im + first_im * twist_re], 2
    )
    return jnp.einsum("ckn,nm->ckm", turned, inner_fwd, precision=PRECISE)


def spectral_product(left, right, conjugate_left):
    width = left.shape[2] // 2
    left_re, left_im = (left[:, :, :width], left[:, :, width:])
    right_re, right_im = (right[:, :, :width], right[:, :, width:])
    if conjugate_left:
        return jnp.concatenate(
            [left_re * right_re + left_im * right_im, left_re * right_im - left_im * right_re], 2
        )
    return jnp.concatenate(
        [left_re * right_re - left_im * right_im, left_re * right_im + left_im * right_re], 2
    )


def inverse_real(spectrum, tables):
    first_table, (twist_re, twist_im), inner_fwd, inner_back, last_table = tables
    blocks = twist_re.shape[0]
    radix_size = twist_re.shape[1]
    undo = jnp.einsum("ckn,nm->ckm", spectrum, inner_back, precision=PRECISE)
    undo_re = undo[:, :, :radix_size]
    undo_im = undo[:, :, radix_size:]
    back = jnp.concatenate(
        [undo_re * twist_re + undo_im * twist_im, undo_im * twist_re - undo_re * twist_im], 1
    )
    result = jnp.einsum("nk,ckm->cnm", last_table, back, precision=PRECISE)
    return result.reshape(spectrum.shape[0], blocks // 2 * radix_size) / (blocks * radix_size)


def body(projected, short_taps, long_filter, skip_gain, out_proj, cotangent):
    tok_rows = projected.shape[0]
    chan_all = projected.shape[1] // 3
    prev_rows = passed_along(projected[tok_rows - 2 :], "context", 1)
    extended = jnp.concatenate([prev_rows, projected], 0).astype(jnp.float32)
    current = extended[2:]
    once_back = extended[1 : tok_rows + 1]
    twice_back = extended[:tok_rows]
    mixed = short_taps[0] * current + short_taps[1] * once_back + short_taps[2] * twice_back
    query = mixed[:, :chan_all].astype(jnp.bfloat16)
    keyed = mixed[:, chan_all : 2 * chan_all].astype(jnp.bfloat16)
    valued = mixed[:, 2 * chan_all :].astype(jnp.bfloat16)
    product = (keyed.astype(jnp.float32) * valued.astype(jnp.float32)).astype(jnp.bfloat16)
    product_chan = lax.all_to_all(product.T, "context", split_axis=0, concat_axis=1, tiled=True)
    seq_len = product_chan.shape[1]
    tables = make_tables(seq_len)
    prod_f = product_chan.astype(jnp.float32)
    filter_spec = forward_spectrum(long_filter, tables)
    prod_spec = forward_spectrum(prod_f, tables)
    long_chan = (
        inverse_real(spectral_product(filter_spec, prod_spec, False), tables)
        + skip_gain[:, None] * prod_f
    )
    long_tok = lax.all_to_all(
        long_chan.astype(jnp.bfloat16), "context", split_axis=1, concat_axis=0, tiled=True
    ).T
    gate = (query.astype(jnp.float32) * long_tok.astype(jnp.float32)).astype(jnp.bfloat16)
    grad_gate = lax.dot_general(
        cotangent,
        lax.all_gather(out_proj, "dp", axis=0, tiled=True),
        (((1,), (1,)), ((), ())),
        preferred_element_type=jnp.float32,
    ).astype(jnp.bfloat16)
    grad_rows = lax.psum_scatter(
        lax.dot_general(
            gate, cotangent, (((0,), (0,)), ((), ())), preferred_element_type=jnp.float32
        ),
        ("dp", "context"),
        scatter_dimension=0,
        tiled=True,
    )
    grad_query = grad_gate.astype(jnp.float32) * long_tok.astype(jnp.float32)
    grad_long = (grad_gate.astype(jnp.float32) * query.astype(jnp.float32)).astype(jnp.bfloat16)
    grad_chan = lax.all_to_all(
        grad_long.T, "context", split_axis=0, concat_axis=1, tiled=True
    ).astype(jnp.float32)
    grad_spec = forward_spectrum(grad_chan, tables)
    back_chan = (
        inverse_real(spectral_product(filter_spec, grad_spec, True), tables)
        + skip_gain[:, None] * grad_chan
    )
    filter_local = inverse_real(spectral_product(prod_spec, grad_spec, True), tables)
    grad_product = lax.all_to_all(
        back_chan.astype(jnp.bfloat16), "context", split_axis=1, concat_axis=0, tiled=True
    ).T
    scale_factor = 1.0 / math.sqrt(seq_len * lax.axis_size("dp"))
    grad_filter = (
        lax.psum_scatter(filter_local, "dp", scatter_dimension=1, tiled=True) * scale_factor
    )
    grad_skip = lax.psum(jnp.sum(grad_chan * prod_f, axis=1), "dp") * scale_factor
    grad_key = grad_product.astype(jnp.float32) * valued.astype(jnp.float32)
    grad_value = grad_product.astype(jnp.float32) * keyed.astype(jnp.float32)
    grad_mixed = jnp.concatenate([grad_query, grad_key, grad_value], 1)
    next_rows = passed_along(grad_mixed[:2].astype(jnp.bfloat16), "context", -1).astype(jnp.float32)
    grad_ext = jnp.concatenate([grad_mixed, next_rows], 0)
    grad_inputs = (
        short_taps[0] * grad_ext[:tok_rows]
        + short_taps[1] * grad_ext[1 : tok_rows + 1]
        + short_taps[2] * grad_ext[2:]
    ).astype(jnp.bfloat16)
    taps_terms = jnp.stack(
        [
            jnp.sum(grad_mixed * current, 0),
            jnp.sum(grad_mixed * once_back, 0),
            jnp.sum(grad_mixed * twice_back, 0),
        ]
    )
    grad_taps = lax.psum(taps_terms, ("dp", "context")) * scale_factor
    return (grad_inputs, grad_taps, grad_filter, grad_skip, grad_rows * scale_factor)


def solution(mesh):
    placed = (
        P(("dp", "context"), None),
        P(),
        P("context", None),
        P("context"),
        P("dp", None),
        P(("dp", "context"), None),
    )
    return jax.shard_map(
        body,
        mesh=mesh,
        in_specs=placed,
        out_specs=(
            P(("dp", "context"), None),
            P(),
            P("context", "dp"),
            P("context"),
            P(("dp", "context"), None),
        ),
        check_vma=False,
    )
```

profile of v0, /device:TPU:0, one launch (start us, length us, event | category | flops | bytes accessed | tf_op | source)
XLA Modules:
  0.0 625.5 jit_solution(3541810269681701199)
XLA Ops:
  15.6 84.6 %all-gather.2.cloned.1.call-done = bf16[2048,2048]{1,0:T(8,128)(2,1)} async-done(((bf16[512,2048]{1,0:T(8,128)(2,1)}), bf16[2048,2048]{1,0:T(8,128)(2,1)}) %all-gather.2.cloned.1.call-update) | async-done | bytes 8388624 | tf_op jit(solution)/shard_map/all_gather | solution.py:112
  100.2 6.2 fusion.21
  108.6 4.6 all-to-all-start.2
  115.5 3.9 convolution_bitcast_fusion.2
  119.5 9.1 %all-to-all-done.2 = bf16[8,256,128]{2,1,0:T(8,128)(2,1)S(1)} async-done(((bf16[8,256,128]{2,1,0:T(8,128)(2,1)}), bf16[8,256,128]{2,1,0:T(8,128)(2,1)S(1)}, u32[]{:S(2)}, u32[]{:S(2)}) %all-to-all-start.2) | async-done | bytes 524320 | tf_op jit(solution)/shard_map/all_to_all | solution.py:126
  132.6 4.2 fusion.16
  136.8 4.2 fusion.12
  145.5 5.5 copy.61
  151.0 4.0 fusion.68
  159.0 17.8 %all_to_all.52 = bf16[256,8,128]{2,0,1:T(8,128)(2,1)S(1)} all-to-all(bf16[256,8,128]{2,0,1:T(8,128)(2,1)S(1)} %copy.52), channel_id=1, replica_groups=mesh['dp'=4,'context'=8] {'context'}, dimensions={1} | all-to-all | bytes 1048576 | tf_op jit(solution)/shard_map/all_to_all | solution.py:135
  181.2 17.8 %all_to_all.53 = bf16[8,256,128]{2,1,0:T(8,128)(2,1)S(1)} all-to-all(bf16[8,256,128]{2,1,0:T(8,128)(2,1)S(1)} %bitcast.96), channel_id=1, replica_groups=mesh['dp'=4,'context'=8] {'context'}, dimensions={0} | all-to-all | bytes 1048576 | tf_op jit(solution)/shard_map/all_to_all | solution.py:96
  202.0 4.1 fusion.14
  206.1 4.4 multiply_add_fusion.1
  210.5 4.6 pad_maximum_fusion.5
  215.1 5.5 copy.64
  220.6 6.1 fusion.66
  229.0 5.6 copy.58
  234.7 4.3 fusion.70
  245.1 17.8 %all_to_all.54 = bf16[256,8,128]{2,0,1:T(8,128)(2,1)S(1)} all-to-all(bf16[256,8,128]{2,0,1:T(8,128)(2,1)S(1)} %copy.43), channel_id=1, replica_groups=mesh['dp'=4,'context'=8] {'context'}, dimensions={1} | all-to-all | bytes 1048576 | tf_op jit(solution)/shard_map/all_to_all | solution.py:106
  282.0 9.1 %fusion.53 = f32[2048,2048]{1,0:T(8,128)} fusion(bf16[128,2048]{1,0:T(8,128)(2,1)S(1)} %copy-done, f32[2048,128]{0,1:T(8,128)S(1)} %copy-done.10, bf16[128,6144]{1,0:T(8,128)(2,1)} %copy-done.12), kind=kOutput, calls=%fused_computation.82 | convolution fusion | flops 1074528256 | bytes 18874368 | tf_op jit(solution)/shard_map/dot_general | solution.py:117
  293.5 8.9 %psum.15 = f32[256]{0:T(256)S(1)} all-reduce(f32[256]{0:T(256)S(1)} %fusion.52), channel_id=1, replica_groups=mesh['dp'=4,'context'=8] {'dp'}, use_global_device_ids=true, to_apply=%region_6.7 | all-reduce | flops 256 | bytes 2048 | tf_op jit(solution)/shard_map/psum | solution.py:142
  303.0 93.5 %all-reduce.2.cloned.1.call-done = f32[3,6144]{1,0:T(4,128)} async-done(((f32[3,6144]{1,0:T(4,128)}), f32[3,6144]{1,0:T(4,128)}) %all-reduce.2.cloned.1.call-update) | async-done | bytes 73744 | tf_op jit(solution)/shard_map/psum | solution.py:160
  398.0 29.9 %reduce-scatter.3.cloned.1.call-done = f32[256,256]{1,0:T(8,128)} async-done(((f32[256,1024]{1,0:T(8,128)}), f32[256,256]{1,0:T(8,128)}) %reduce-scatter.3.cloned.1.call-update) | async-done | bytes 262160 | tf_op jit(solution)/shard_map/reduce_scatter | solution.py:140
  429.6 187.3 %reduce-scatter.5.cloned.1.call-done = f32[64,2048]{1,0:T(8,128)} async-done(((f32[2048,2048]{1,0:T(8,128)}), f32[64,2048]{1,0:T(8,128)}) %reduce-scatter.5.cloned.1.call-update) | async-done | bytes 524304 | tf_op jit(solution)/shard_map/reduce_scatter | solution.py:116
  (108 shorter events, 67.9 us)
Async XLA Ops:
  7.2 93.1 %copy-start = (bf16[128,2048]{1,0:T(8,128)(2,1)S(1)}, bf16[128,2048]{1,0:T(8,128)(2,1)}, u32[]{:S(2)}) copy-start(bf16[128,2048]{1,0:T(8,128)(2,1)} %param.11) | copy-start | bytes 1572868
  7.2 5.3 copy-start.20
  7.2 93.0 %all-gather.2.cloned.1.call-start = ((), (), s32[]{:S(2)}) async-start(), calls=%async_computation.6 | async-start | bytes 10485760 | tf_op jit(solution)/shard_map/all_gather | solution.py:112
  8.8 3.6 collective-permute-start
  12.9 1.7 copy-start.1
  15.6 90.9 %copy-start.12 = (bf16[128,6144]{1,0:T(8,128)(2,1)}, bf16[128,6144]{1,0:T(8,128)(2,1)S(1)}, u32[]{:S(2)}) copy-start(bf16[128,6144]{1,0:T(8,128)(2,1)S(1)} %add_convert_fusion) | copy-start | bytes 4718596
  108.6 20.0 %all-to-all-start.2 = ((bf16[8,256,128]{2,1,0:T(8,128)(2,1)}), bf16[8,256,128]{2,1,0:T(8,128)(2,1)S(1)}, u32[]{:S(2)}, u32[]{:S(2)}) async-start(bf16[8,256,128]{2,1,0:T(8,128)(2,1)} %bitcast.17), calls=%async_computation.2 | async-start | bytes 1048576 | tf_op jit(solution)/shard_map/all_to_all | solution.py:126
  113.2 283.3 %all-reduce.2.cloned.1.call-start = ((), (), s32[]{:S(2)}) async-start(), calls=%async_computation.7 | async-start | bytes 196608 | tf_op jit(solution)/shard_map/psum | solution.py:160
  128.6 26.9 %copy-start.13 = (bf16[8,256,128]{2,1,0:T(8,128)(2,1)}, bf16[8,256,128]{2,1,0:T(8,128)(2,1)S(1)}, u32[]{:S(2)}) copy-start(bf16[8,256,128]{2,1,0:T(8,128)(2,1)S(1)} %all-to-all-done.2) | copy-start | bytes 1572868
  128.6 2.4 copy-start.7
  136.8 4.2 copy-start.3
  141.0 1.9 copy-start.5
  201.9 4.1 copy-start.4
  202.0 4.1 copy-start.6
  220.6 6.1 copy-start.18
  220.6 6.1 copy-start.19
  234.7 4.3 copy-start.8
  239.0 2.8 copy-start.16
  262.9 5.3 copy-start.9
  268.4 3.1 collective-permute-start.1
  271.5 1.9 copy-start.2
  277.2 150.8 %reduce-scatter.3.cloned.1.call-start = ((), (), s32[]{:S(2)}) async-start(), calls=%async_computation.8 | async-start | bytes 1310720 | tf_op jit(solution)/shard_map/reduce_scatter | solution.py:140
  277.3 4.8 copy-start.10
  282.0 334.9 %reduce-scatter.5.cloned.1.call-start = ((), (), s32[]{:S(2)}) async-start(), calls=%async_computation.9 | async-start | bytes 17301504 | tf_op jit(solution)/shard_map/reduce_scatter | solution.py:116
  (5 other events, 4.7 us)
Sparse Core Ops, SparseCore 0:
  9.9 90.2 all-gather.1
  277.3 119.1 all-reduce.1
  399.4 28.5 reduce-scatter.2
  430.2 186.6 reduce-scatter.4
where the time goes:
time: 631 us; the launch traced here: 626 us
  waiting for transfers between devices  407 us (65%)
  blocking collectives  62.2 us (10%)
  matrix products  58.9 us (9%)
  other arithmetic  39.3 us (6%)
  local copies, waits for them, and re-layouts  35.3 us (6%)
  between operations  14.5 us (2%)
  starting transfers between devices  8.42 us (1%)
    reduce_scatter x1, waiting for transfers between devices, body(): lax.psum_scatter(lax.dot_general(gate, cotangent, (((0,), (0,)), ((), ())...  187 us
    psum x1, waiting for transfers between devices, body(): grad_taps = lax.psum(taps_terms, ('dp', 'context')) * scale_factor  93.5 us
    all_gather x1, waiting for transfers between devices, body(): lax.all_gather(out_proj, 'dp', axis=0, tiled=True)  84.6 us
    reduce_scatter x1, waiting for transfers between devices, body(): lax.psum_scatter(filter_local, 'dp', scatter_dimension=1, tiled=True)  29.9 us
    all_to_all x1, blocking collectives, body(): lax.all_to_all(back_chan.astype(jnp.bfloat16), 'context', split_axis=1, c...  17.8 us
    all_to_all x1, blocking collectives, body(): lax.all_to_all(product.T, 'context', split_axis=0, concat_axis=1, tiled=T...  17.8 us
    all_to_all x1, blocking collectives, body(): lax.all_to_all(long_chan.astype(jnp.bfloat16), 'context', split_axis=1, c...  17.8 us
    dot_general x3, matrix products, inverse_real(): undo = jnp.einsum('ckn,nm->ckm', spectrum, inner_back, precision=PRECISE)  14.4 us
  transfers between devices with their start and end apart: 7, of which 6 were waited for; matrix products, arithmetic and copies ran while one was open for 5% of the time, Pallas kernels for 0%

commit v1 on v0

--- a/solution.py
+++ b/solution.py
@@ -157,7 +157,7 @@
             jnp.sum(grad_mixed * twice_back, 0),
         ]
     )
-    grad_taps = lax.psum(taps_terms, ("dp", "context")) * scale_factor
+    grad_taps = jnp.sum(lax.all_gather(taps_terms, ("dp", "context")), axis=0) * scale_factor
     return (grad_inputs, grad_taps, grad_filter, grad_skip, grad_rows * scale_factor)
 
 

time: 631 us -> 563 us (0.89)
  waiting for transfers between devices: 407 us -> 339 us
    psum x1 -> x0, waiting for transfers between devices: 93.5 us -> none  [body(): grad_taps = lax.psum(taps_terms, ('dp', 'context')) * scale_factor]
    all_gather x0 -> x1, waiting for transfers between devices: none -> 60.3 us  [body(): lax.all_gather(taps_terms, ('dp', 'context'))]
    reduce_scatter x1, waiting for transfers between devices: 29.9 us -> 0.01 us  [body(): lax.psum_scatter(filter_local, 'dp', scatter_dimension=1, tiled=True)]
  transfers between devices with their start and end apart: 7 -> 7, of which waited for: 6 -> 4; matrix products, arithmetic and copies ran while one was open for 5% -> 6% of each run, Pallas kernels for 0% -> 0%
where the time goes in v1:
time: 563 us; the launch traced here: 557 us
  waiting for transfers between devices  339 us (60%)
  blocking collectives  62.4 us (11%)
  matrix products  57 us (10%)
  other arithmetic  42.5 us (8%)
  local copies, waits for them, and re-layouts  33.3 us (6%)
  between operations  14.5 us (3%)
  starting transfers between devices  8.42 us (1%)
    reduce_scatter x1, waiting for transfers between devices, body(): lax.psum_scatter(lax.dot_general(gate, cotangent, (((0,), (0,)), ((), ())...  185 us
    all_gather x1, waiting for transfers between devices, body(): lax.all_gather(out_proj, 'dp', axis=0, tiled=True)  84.6 us
    all_gather x1, waiting for transfers between devices, body(): lax.all_gather(taps_terms, ('dp', 'context'))  60.3 us
    all_to_all x1, blocking collectives, body(): lax.all_to_all(back_chan.astype(jnp.bfloat16), 'context', split_axis=1, c...  17.8 us
    all_to_all x1, blocking collectives, body(): lax.all_to_all(product.T, 'context', split_axis=0, concat_axis=1, tiled=T...  17.8 us
    all_to_all x1, blocking collectives, body(): lax.all_to_all(long_chan.astype(jnp.bfloat16), 'context', split_axis=1, c...  17.8 us
    dot_general x3, matrix products, inverse_real(): undo = jnp.einsum('ckn,nm->ckm', spectrum, inner_back, precision=PRECISE)  14.4 us
    dot_general x3, matrix products, forward_spectrum(): return jnp.einsum('ckn,nm->ckm', turned, inner_fwd, precision=PRECISE)  12.5 us
  transfers between devices with their start and end apart: 7, of which 4 were waited for; matrix products, arithmetic and copies ran while one was open for 6% of the time, Pallas kernels for 0%

profile of v1, /device:TPU:0, one launch (start us, length us, event | category | flops | bytes accessed | tf_op | source)
XLA Modules:
  0.0 557.5 jit_solution(2613631138877257890)
XLA Ops:
  15.6 84.6 %all-gather.5.cloned.1.call-done = bf16[2048,2048]{1,0:T(8,128)(2,1)} async-done(((bf16[512,2048]{1,0:T(8,128)(2,1)}), bf16[2048,2048]{1,0:T(8,128)(2,1)}) %all-gather.5.cloned.1.call-update) | async-done | bytes 8388624 | tf_op jit(solution)/shard_map/all_gather | solution.py:112
  100.2 6.2 %fusion.21 = f32[128,2048]{1,0:T(8,128)S(1)} fusion(bf16[128,2048]{1,0:T(8,128)(2,1)S(1)} %copy-done, bf16[2048,2048]{1,0:T(8,128)(2,1)} %all-gather.5.cloned.1.call-done), kind=kOutput, calls=%fused_computation.36 | convolution fusion | flops 1074266112 | bytes 9961472 | tf_op jit(solution)/shard_map/dot_general | solution.py:110
  108.6 4.6 all-to-all-start.2
  115.5 3.9 convolution_bitcast_fusion.2
  119.5 9.1 %all-to-all-done.2 = bf16[8,256,128]{2,1,0:T(8,128)(2,1)S(1)} async-done(((bf16[8,256,128]{2,1,0:T(8,128)(2,1)}), bf16[8,256,128]{2,1,0:T(8,128)(2,1)S(1)}, u32[]{:S(2)}, u32[]{:S(2)}) %all-to-all-start.2) | async-done | bytes 524320 | tf_op jit(solution)/shard_map/all_to_all | solution.py:126
  132.6 4.2 fusion.16
  136.8 4.2 fusion.12
  145.5 5.5 copy.61
  151.0 4.0 fusion.68
  159.0 17.8 %all_to_all.52 = bf16[256,8,128]{2,0,1:T(8,128)(2,1)S(1)} all-to-all(bf16[256,8,128]{2,0,1:T(8,128)(2,1)S(1)} %copy.52), channel_id=1, replica_groups=mesh['dp'=4,'context'=8] {'context'}, dimensions={1} | all-to-all | bytes 1048576 | tf_op jit(solution)/shard_map/all_to_all | solution.py:135
  181.2 17.8 %all_to_all.53 = bf16[8,256,128]{2,1,0:T(8,128)(2,1)S(1)} all-to-all(bf16[8,256,128]{2,1,0:T(8,128)(2,1)S(1)} %bitcast.98), channel_id=1, replica_groups=mesh['dp'=4,'context'=8] {'context'}, dimensions={0} | all-to-all | bytes 1048576 | tf_op jit(solution)/shard_map/all_to_all | solution.py:96
  202.0 4.1 fusion.14
  206.1 4.4 multiply_add_fusion.1
  210.5 4.6 pad_maximum_fusion.5
  215.1 5.5 copy.64
  220.6 6.1 %fusion.66 = f32[256,16,256]{2,1,0:T(8,128)} fusion(f32[256,16,256]{2,1,0:T(8,128)} %copy.64, f32[128,128]{0,1:T(8,128)S(1)} %get-tuple-element.42, f32[128,128]{0,1:T(8,128)S(1)} %get-tuple-element.41, f32[128,128]{0,1:T(8,128)S(1)} %fusion.83), kind=kOutput, calls=%fused_computation.99 | convolution fusion | flops 1610809344 | bytes 8585216 | tf_op jit(solution)/shard_map/ckn,nm->ckm/dot_general | solution.py:73
  229.0 5.6 %copy.58 = f32[256,16,256]{2,1,0:T(8,128)} copy(f32[256,16,256]{0,2,1:T(8,128)} %pad_maximum_fusion.2) | data formatting | bytes 8388608 | tf_op jit(solution)/shard_map/concatenate | solution.py:64
  234.7 4.3 fusion.70
  241.8 3.2 fusion.43
  245.1 17.8 %all_to_all.54 = bf16[256,8,128]{2,0,1:T(8,128)(2,1)S(1)} all-to-all(bf16[256,8,128]{2,0,1:T(8,128)(2,1)S(1)} %copy.43), channel_id=1, replica_groups=mesh['dp'=4,'context'=8] {'context'}, dimensions={1} | all-to-all | bytes 1048576 | tf_op jit(solution)/shard_map/all_to_all | solution.py:106
  277.7 9.5 %fusion.53 = f32[2048,2048]{1,0:T(8,128)} fusion(bf16[128,2048]{1,0:T(8,128)(2,1)S(1)} %copy-done, f32[2048,128]{0,1:T(8,128)} %copy.70, bf16[128,6144]{1,0:T(8,128)(2,1)} %copy-done.11), kind=kOutput, calls=%fused_computation.82 | convolution fusion | flops 1074528256 | bytes 18874368 | tf_op jit(solution)/shard_map/dot_general | solution.py:117
  289.6 9.1 %psum.7 = f32[256]{0:T(256)S(1)} all-reduce(f32[256]{0:T(256)S(1)} %fusion.52), channel_id=1, replica_groups=mesh['dp'=4,'context'=8] {'dp'}, use_global_device_ids=true, to_apply=%region_6.7 | all-reduce | flops 256 | bytes 2048 | tf_op jit(solution)/shard_map/psum | solution.py:142
  300.9 60.3 %all-gather.7.cloned.1.call-done = f32[32,3,6144]{2,1,0:T(4,128)} async-done(((f32[1,3,6144]{2,1,0:T(4,128)}), f32[32,3,6144]{2,1,0:T(4,128)}) %all-gather.7.cloned.1.call-update) | async-done | bytes 2359312 | tf_op jit(solution)/shard_map/all_gather | solution.py:160
  364.2 184.7 %reduce-scatter.5.cloned.1.call-done = f32[64,2048]{1,0:T(8,128)} async-done(((f32[2048,2048]{1,0:T(8,128)}), f32[64,2048]{1,0:T(8,128)}) %reduce-scatter.5.cloned.1.call-update) | async-done | bytes 524304 | tf_op jit(solution)/shard_map/reduce_scatter | solution.py:116
  (111 shorter events, 61.8 us)
Async XLA Ops:
  7.2 93.1 %copy-start = (bf16[128,2048]{1,0:T(8,128)(2,1)S(1)}, bf16[128,2048]{1,0:T(8,128)(2,1)}, u32[]{:S(2)}) copy-start(bf16[128,2048]{1,0:T(8,128)(2,1)} %param.11) | copy-start | bytes 1572868
  7.2 5.3 copy-start.21
  7.2 93.0 %all-gather.5.cloned.1.call-start = ((), (), s32[]{:S(2)}) async-start(), calls=%async_computation.6 | async-start | bytes 10485760 | tf_op jit(solution)/shard_map/all_gather | solution.py:112
  8.8 3.6 collective-permute-start
  15.6 90.9 %copy-start.11 = (bf16[128,6144]{1,0:T(8,128)(2,1)}, bf16[128,6144]{1,0:T(8,128)(2,1)S(1)}, u32[]{:S(2)}) copy-start(bf16[128,6144]{1,0:T(8,128)(2,1)S(1)} %add_convert_fusion) | copy-start | bytes 4718596
  108.6 20.0 %all-to-all-start.2 = ((bf16[8,256,128]{2,1,0:T(8,128)(2,1)}), bf16[8,256,128]{2,1,0:T(8,128)(2,1)S(1)}, u32[]{:S(2)}, u32[]{:S(2)}) async-start(bf16[8,256,128]{2,1,0:T(8,128)(2,1)} %bitcast.17), calls=%async_computation.2 | async-start | bytes 1048576 | tf_op jit(solution)/shard_map/all_to_all | solution.py:126
  113.2 186.0 %reduce-scatter.3.cloned.1.call-start = ((), (), s32[]{:S(2)}) async-start(), calls=%async_computation.7 | async-start | bytes 1310720 | tf_op jit(solution)/shard_map/reduce_scatter | solution.py:140
  128.6 26.9 %copy-start.14 = (bf16[8,256,128]{2,1,0:T(8,128)(2,1)}, bf16[8,256,128]{2,1,0:T(8,128)(2,1)S(1)}, u32[]{:S(2)}) copy-start(bf16[8,256,128]{2,1,0:T(8,128)(2,1)S(1)} %all-to-all-done.2) | copy-start | bytes 1572868
  128.6 2.4 copy-start.7
  136.8 4.2 copy-start.3
  141.0 1.9 copy-start.5
  201.9 4.1 copy-start.4
  201.9 4.1 copy-start.6
  220.6 6.1 %copy-start.19 = (f32[256,16,128]{0,2,1:T(8,128)S(1)}, f32[256,16,128]{0,2,1:T(8,128)}, u32[]{:S(2)}) copy-start(f32[256,16,128]{0,2,1:T(8,128)} %get-tuple-element.26) | copy-start | bytes 6291460
  220.6 6.1 %copy-start.20 = (f32[256,16,128]{0,2,1:T(8,128)S(1)}, f32[256,16,128]{0,2,1:T(8,128)}, u32[]{:S(2)}) copy-start(f32[256,16,128]{0,2,1:T(8,128)} %get-tuple-element.27) | copy-start | bytes 6291460
  234.7 4.3 copy-start.8
  239.0 2.8 copy-start.17
  265.9 2.9 copy-start.12
  266.0 2.9 copy-start.13
  267.6 3.8 collective-permute-start.1
  271.3 89.8 %all-gather.7.cloned.1.call-start = ((), (), s32[]{:S(2)}) async-start(), calls=%async_computation.9 | async-start | bytes 3244032 | tf_op jit(solution)/shard_map/all_gather | solution.py:160
  271.4 2.3 copy-start.2
  271.4 2.5 copy-start.9
  277.7 271.2 %reduce-scatter.5.cloned.1.call-start = ((), (), s32[]{:S(2)}) async-start(), calls=%async_computation.8 | async-start | bytes 17301504 | tf_op jit(solution)/shard_map/reduce_scatter | solution.py:116
  (6 other events, 6.4 us)
Sparse Core Ops, SparseCore 0:
  9.9 90.2 all-gather.4
  271.4 26.5 reduce-scatter.2
  302.0 59.0 all-gather.6
  363.4 185.4 reduce-scatter.4
